TPU v7x, 32 devices: a whole 2x2x4 slice. The times are simulated.
32 devices in a mesh: groups: 2 (over y), ctx: 4 (over z), wt: 2 (over x), sub: 2 (over core).
Axes of the slice: x: 2, y: 2, z: 4, core: 2. Of those that a mesh axis runs over, the one named last changes fastest.
Arguments:
- queries: bfloat16 [16, 32, 128, 576], P(('groups', 'ctx'), None, ('wt', 'sub')), parts along dimension 0, may hold values from -80 to 80
- selection: int32 [16, 4, 2], P(('groups', 'ctx')), parts along dimension 0, may hold values from -1 to 15, as said below
- latent_cache: bfloat16 [128, 64, 576], P(('groups', 'ctx')), parts along dimension 0, may hold values from -8 to 8
- value_up: bfloat16 [128, 512, 128], P(None, ('wt', 'sub')), may hold values from -1 to 1
Outputs:
- attended: bfloat16 [16, 32, 128, 128], P(('groups', 'ctx'), None, ('wt', 'sub')), parts along dimension 0
There are 2 independent parts, one for each index of `groups`. A program takes and returns all parts, laid end to end along the dimension named above; an argument that names none is the same for every part. Nothing has to cross between parts.
Inputs may be any that keep to these rules, and one draw needn't show every extreme that they name: `selection`: entry [c, o, s] is the number of a block among the 16 of owner o, or -1 for an empty slot; in an owner's slots live entries come first and differ. Each query block has 4 live entries in all, and in every query block some owner fills all 2 slots.
All inputs are finite; a program needn't handle non-finite values.
Results may differ from a plain program's by a relative error of at most 0.008.
Values may be sent and summed in bfloat16 or wider, within the bound.
No kernel may reach another device: no remote copies, remote signals or barrier semaphores. Data moves between devices by JAX's collectives and lax.ppermute only.
A program may use at most 128 MiB of HBM per device.

v0:
```python
import jax
import jax.numpy as jnp
from jax import lax
from jax.sharding import PartitionSpec as P

LAT = 512
ROPE = 64
NOPE = 128


def attend(query, blocks, chosen):
    width = query.shape[2]
    owners = chosen.shape[0]
    count = chosen.shape[0] * chosen.shape[1]
    live = (chosen >= 0).reshape(-1)
    ranked = jnp.where(live, 0, count).astype(jnp.int32) + jnp.arange(count, dtype=jnp.int32)
    picked = jnp.argsort(ranked)[:owners]
    keys = blocks.reshape(count, blocks.shape[2], width)[picked].reshape(-1, width)
    rows = query.reshape(-1, width)
    scores = jnp.einsum("rd,kd->rk", rows, keys, preferred_element_type=jnp.float32)
    scores = scores * jnp.float32((NOPE + ROPE) ** (-0.5))
    expo = jnp.exp(scores - jnp.max(scores, axis=1, keepdims=True))
    totals = jnp.sum(expo, axis=1, keepdims=True)
    weights = expo.astype(jnp.bfloat16)
    latent = (jnp.dot(weights, keys[:, :LAT], preferred_element_type=jnp.float32) / totals).astype(
        jnp.bfloat16
    )
    return latent.reshape(query.shape[0], query.shape[1], LAT)


def per_device(queries, selection, latent_cache, value_up):
    owners = lax.axis_size("ctx")
    spans, per_span, heads_here, width = queries.shape
    slots = selection.shape[2]
    block_len = latent_cache.shape[1]

    def serve(asked):
        safe = jnp.clip(asked, 0, latent_cache.shape[0] - 1)
        return lax.all_to_all(latent_cache[safe], "ctx", split_axis=0, concat_axis=0, tiled=True)

    def fetch(wanted):
        half = slots // 2
        mine = lax.dynamic_slice_in_dim(wanted, lax.axis_index("sub") * half, half, 2)
        count = mine.shape[1] * mine.shape[2]
        fetched = serve(
            lax.all_to_all(
                mine.reshape(owners, count), "ctx", split_axis=0, concat_axis=0, tiled=True
            )
        )
        fetched = fetched.reshape(owners, mine.shape[1], mine.shape[2], block_len, width)
        fetched = lax.all_gather(fetched, "sub", axis=2, tiled=True)
        return fetched

    wanted_all = jnp.transpose(selection, (1, 0, 2))
    gathered = [fetch(wanted_all[:, index : index + 1])[:, 0] for index in range(spans)]
    latents = [attend(queries[index], gathered[index], selection[index]) for index in range(spans)]
    flat = jnp.stack(latents).reshape(spans * per_span, heads_here, LAT)
    my_weights = lax.all_to_all(value_up, ("wt", "sub"), split_axis=0, concat_axis=1, tiled=True)
    summed = jnp.einsum("nhl,hlv->nhv", flat, my_weights, preferred_element_type=jnp.float32)
    return summed.astype(jnp.bfloat16).reshape(spans, per_span, heads_here, my_weights.shape[2])


def solution(mesh):
    placed = (
        P(("groups", "ctx"), None, ("wt", "sub"), None),
        P(("groups", "ctx"), None, None),
        P(("groups", "ctx"), None, None),
        P(None, ("wt", "sub"), None),
    )
    return jax.shard_map(
        per_device,
        mesh=mesh,
        in_specs=placed,
        out_specs=P(("groups", "ctx"), None, ("wt", "sub"), None),
        check_vma=False,
    )
```

profile of v0, /device:TPU:0, one launch (start us, length us, event | category | flops | bytes accessed | tf_op | source)
XLA Modules:
  0.0 102.0 jit_solution(10457877809274622)
XLA Ops:
  0.0 0.0 copy-start
  0.0 0.9 copy.21
  0.9 0.7 constant_dynamic-slice_fusion.1
  1.6 6.3 %all-to-all-start = ((s32[4,1,1]{2,1,0:T(1,128)}), s32[4,1,1]{2,1,0:T(1,128)S(1)}, u32[]{:S(2)}, u32[]{:S(2)}) async-start(s32[4,1,1]{2,1,0:T(1,128)} %constant_dynamic-slice_fusion.1), calls=%async_computation | async-start | bytes 4096 | tf_op jit(solution)/shard_map/all_to_all | solution.py:46
  7.9 0.7 constant_dynamic-slice_fusion
  8.6 4.8 %all-to-all-done = s32[4,1,1]{2,1,0:T(1,128)S(1)} async-done(((s32[4,1,1]{2,1,0:T(1,128)}), s32[4,1,1]{2,1,0:T(1,128)S(1)}, u32[]{:S(2)}, u32[]{:S(2)}) %all-to-all-start) | async-done | bytes 48 | tf_op jit(solution)/shard_map/all_to_all | solution.py:46
  13.3 3.2 %all-to-all-start.2 = ((s32[4,1,1]{2,1,0:T(1,128)}), s32[4,1,1]{2,1,0:T(1,128)S(1)}, u32[]{:S(2)}, u32[]{:S(2)}) async-start(s32[4,1,1]{2,1,0:T(1,128)} %constant_dynamic-slice_fusion), calls=%async_computation.2 | async-start | bytes 4096 | tf_op jit(solution)/shard_map/all_to_all | solution.py:46
  16.6 0.2 fusion.10
  16.7 0.0 copy-done
  16.7 1.3 %gather_fusion = bf16[4,64,576]{2,1,0:T(8,128)(2,1)} fusion(bf16[16,64,576]{2,1,0:T(8,128)(2,1)S(1)} %copy-done, s32[1024]{0:T(1024)S(1)} %pad_clamp_fusion.3), kind=kCustom, calls=%fused_computation | custom fusion | bytes 589840 | tf_op jit(solution)/shard_map/gather | solution.py:39
  18.0 4.0 %all-to-all-done.2 = s32[4,1,1]{2,1,0:T(1,128)S(1)} async-done(((s32[4,1,1]{2,1,0:T(1,128)}), s32[4,1,1]{2,1,0:T(1,128)S(1)}, u32[]{:S(2)}, u32[]{:S(2)}) %all-to-all-start.2) | async-done | bytes 48 | tf_op jit(solution)/shard_map/all_to_all | solution.py:46
  22.0 3.5 %all-to-all-start.1 = ((bf16[4,1,64,576]{3,2,1,0:T(8,128)(2,1)}), bf16[4,1,64,576]{3,2,1,0:T(8,128)(2,1)S(1)}, u32[]{:S(2)}, u32[]{:S(2)}) async-start(bf16[4,1,64,576]{3,2,1,0:T(8,128)(2,1)} %bitcast.1), calls=%async_computation.1 | async-start | bytes 655360 | tf_op jit(solution)/shard_map/all_to_all | solution.py:39
  25.5 0.2 fusion.11
  25.7 1.3 %gather_fusion.2 = bf16[4,64,576]{2,1,0:T(8,128)(2,1)} fusion(bf16[16,64,576]{2,1,0:T(8,128)(2,1)S(1)} %copy-done, s32[1024]{0:T(1024)S(1)} %pad_clamp_fusion.1), kind=kCustom, calls=%fused_computation.2 | custom fusion | bytes 589840 | tf_op jit(solution)/shard_map/gather | solution.py:39
  27.0 5.8 %all-to-all-done.1 = bf16[4,1,64,576]{3,2,1,0:T(8,128)(2,1)S(1)} async-done(((bf16[4,1,64,576]{3,2,1,0:T(8,128)(2,1)}), bf16[4,1,64,576]{3,2,1,0:T(8,128)(2,1)S(1)}, u32[]{:S(2)}, u32[]{:S(2)}) %all-to-all-start.1) | async-done | bytes 294944 | tf_op jit(solution)/shard_map/all_to_all | solution.py:39
  32.8 3.6 %all-to-all-start.3 = ((bf16[4,1,64,576]{3,2,1,0:T(8,128)(2,1)}), bf16[4,1,64,576]{3,2,1,0:T(8,128)(2,1)S(1)}, u32[]{:S(2)}, u32[]{:S(2)}) async-start(bf16[4,1,64,576]{3,2,1,0:T(8,128)(2,1)} %bitcast.6), calls=%async_computation.3 | async-start | bytes 655360 | tf_op jit(solution)/shard_map/all_to_all | solution.py:39
  36.4 0.1 copy.22
  36.5 0.1 select_n.38
  36.5 0.1 copy.23
  36.6 0.1 select_n.42
  36.7 6.9 %all-to-all-done.3 = bf16[4,1,64,576]{3,2,1,0:T(8,128)(2,1)S(1)} async-done(((bf16[4,1,64,576]{3,2,1,0:T(8,128)(2,1)}), bf16[4,1,64,576]{3,2,1,0:T(8,128)(2,1)S(1)}, u32[]{:S(2)}, u32[]{:S(2)}) %all-to-all-start.3) | async-done | bytes 294944 | tf_op jit(solution)/shard_map/all_to_all | solution.py:39
  43.7 0.0 copy-done.1
  43.7 0.7 copy-done.2
  44.4 4.9 %all-to-all-start.4 = ((bf16[128,128,128]{2,1,0:T(8,128)(2,1)}), bf16[128,128,128]{2,1,0:T(8,128)(2,1)}, u32[]{:S(2)}, u32[]{:S(2)}) async-start(bf16[128,128,128]{2,1,0:T(8,128)(2,1)} %param.7), calls=%async_computation.4 | async-start | bytes 8388608 | tf_op jit(solution)/shard_map/all_to_all | solution.py:58
  49.3 1.0 sort.31
  50.2 1.0 sort.32
  51.3 0.0 copy-start.3
  51.3 3.1 %fusion.12 = (bf16[1,32,32,576]{3,2,1,0:T(8,128)(2,1)S(1)}, bf16[1,32,32,576]{3,2,1,0:T(8,128)(2,1)}) fusion(bf16[2,32,32,576]{3,2,1,0:T(8,128)(2,1)} %param.4), kind=kLoop, calls=%fused_computation.36 | loop fusion | bytes 4718592 | tf_op jit(solution)/shard_map/slice | solution.py:56
  54.4 0.0 copy-done.3
  54.4 2.3 %all-gather.1 = bf16[4,2,64,576]{3,2,1,0:T(8,128)(2,1)S(1)} all-gather(bf16[4,1,64,576]{3,2,1,0:T(8,128)(2,1)S(1)} %copy-done.3), channel_id=3, replica_groups=mesh['groups'=2,'ctx'=4,'wt'=2,'sub'=2] {'sub'}, dimensions={1}, use_global_device_ids=true | all-gather | bytes 884736 | tf_op jit(solution)/shard_map/all_gather | solution.py:51
  56.7 1.3 %gather_fusion.3 = bf16[4,64,576]{2,1,0:T(8,128)(2,1)} fusion(bf16[8,64,576]{2,1,0:T(8,128)(2,1)S(1)} %bitcast.30, s32[1024]{0:T(1024)S(1)} %pad_clamp_fusion), kind=kCustom, calls=%fused_computation.3 | custom fusion | bytes 589840 | tf_op jit(solution)/shard_map/gather | solution.py:18
  58.0 2.5 %all-gather = bf16[4,2,64,576]{3,2,1,0:T(8,128)(2,1)S(1)} all-gather(bf16[4,1,64,576]{3,2,1,0:T(8,128)(2,1)} %copy-done.1), channel_id=2, replica_groups=mesh['groups'=2,'ctx'=4,'wt'=2,'sub'=2] {'sub'}, dimensions={1}, use_global_device_ids=true | all-gather | bytes 884736 | tf_op jit(solution)/shard_map/all_gather | solution.py:51
  60.5 1.3 %gather_fusion.1 = bf16[4,64,576]{2,1,0:T(8,128)(2,1)} fusion(bf16[8,64,576]{2,1,0:T(8,128)(2,1)S(1)} %bitcast.31, s32[1024]{0:T(1024)S(1)} %pad_clamp_fusion.2), kind=kCustom, calls=%fused_computation.1 | custom fusion | bytes 589840 | tf_op jit(solution)/shard_map/gather | solution.py:18
  61.8 2.1 %fusion.14 = (f32[1024]{0:T(1024)S(1)}, f32[256,1024]{1,0:T(8,128)S(1)}) fusion(bf16[256,576]{1,0:T(8,128)(2,1)} %bitcast.32, bf16[1024,576]{1,0:T(8,128)(2,1)} %bitcast.28), kind=kOutput, calls=%fused_computation.38 | convolution fusion | flops 302513152 | bytes 2527232 | tf_op jit(solution)/shard_map/rd,kd->rk/dot_general | solution.py:20
  63.9 0.2 fusion.2
  64.1 0.0 copy-start.4
  64.1 0.0 copy-done.5
  64.1 0.6 fusion.15
  64.7 0.2 fusion
  64.9 0.1 copy-done.4
  65.0 0.5 divide_convert_fusion
  65.5 0.5 divide_convert_fusion.1
  66.1 0.2 pad_maximum_fusion
  66.3 1.2 %copy.24 = bf16[2,32,32,512]{3,1,0,2:T(8,128)(2,1)S(1)} copy(bf16[2,32,32,512]{3,2,1,0:T(8,128)(2,1)S(1)} %pad_maximum_fusion) | data formatting | bytes 4194304 | tf_op jit(solution)/shard_map/stack | solution.py:57
  67.4 30.0 %all-to-all-done.4 = bf16[128,128,128]{2,1,0:T(8,128)(2,1)} async-done(((bf16[128,128,128]{2,1,0:T(8,128)(2,1)}), bf16[128,128,128]{2,1,0:T(8,128)(2,1)}, u32[]{:S(2)}, u32[]{:S(2)}) %all-to-all-start.4) | async-done | bytes 4194336 | tf_op jit(solution)/shard_map/all_to_all | solution.py:58
  97.5 2.5 %copy.25 = bf16[4,32,128,128]{3,2,0,1:T(8,128)(2,1)S(1)} copy(bf16[4,32,128,128]{3,2,1,0:T(8,128)(2,1)} %bitcast.12) | data formatting | bytes 8388608 | tf_op jit(solution)/shard_map/all_to_all | solution.py:58
  100.0 0.9 convolution_convert_fusion
  100.8 1.1 %copy.26 = bf16[2,32,32,128]{3,2,1,0:T(8,128)(2,1)} copy(bf16[2,32,32,128]{3,1,0,2:T(8,128)(2,1)S(1)} %bitcast.29) | data formatting | bytes 1048576 | tf_op jit(solution)/shard_map/reshape | solution.py:60
  (17 shorter events, 0.1 us)
Async XLA Ops:
  0.0 16.7 %copy-start = (bf16[16,64,576]{2,1,0:T(8,128)(2,1)S(1)}, bf16[16,64,576]{2,1,0:T(8,128)(2,1)}, u32[]{:S(2)}) copy-start(bf16[16,64,576]{2,1,0:T(8,128)(2,1)} %param.6) | copy-start | bytes 3538948
  0.0 36.4 %copy-start.6 = (s32[2,4,2]{1,2,0:T(2,128)S(1)}, s32[2,4,2]{1,2,0:T(2,128)}, u32[]{:S(2)}) copy-start(s32[2,4,2]{1,2,0:T(2,128)} %param.5) | copy-start | bytes 196
  1.6 11.8 %all-to-all-start = ((s32[4,1,1]{2,1,0:T(1,128)}), s32[4,1,1]{2,1,0:T(1,128)S(1)}, u32[]{:S(2)}, u32[]{:S(2)}) async-start(s32[4,1,1]{2,1,0:T(1,128)} %constant_dynamic-slice_fusion.1), calls=%async_computation | async-start | bytes 4096 | tf_op jit(solution)/shard_map/all_to_all | solution.py:46
  13.3 8.7 %all-to-all-start.2 = ((s32[4,1,1]{2,1,0:T(1,128)}), s32[4,1,1]{2,1,0:T(1,128)S(1)}, u32[]{:S(2)}, u32[]{:S(2)}) async-start(s32[4,1,1]{2,1,0:T(1,128)} %constant_dynamic-slice_fusion), calls=%async_computation.2 | async-start | bytes 4096 | tf_op jit(solution)/shard_map/all_to_all | solution.py:46
  22.0 10.7 %all-to-all-start.1 = ((bf16[4,1,64,576]{3,2,1,0:T(8,128)(2,1)}), bf16[4,1,64,576]{3,2,1,0:T(8,128)(2,1)S(1)}, u32[]{:S(2)}, u32[]{:S(2)}) async-start(bf16[4,1,64,576]{3,2,1,0:T(8,128)(2,1)} %bitcast.1), calls=%async_computation.1 | async-start | bytes 655360 | tf_op jit(solution)/shard_map/all_to_all | solution.py:39
  32.8 10.9 %copy-start.1 = (bf16[4,1,64,576]{3,2,1,0:T(8,128)(2,1)}, bf16[4,1,64,576]{3,2,1,0:T(8,128)(2,1)S(1)}, u32[]{:S(2)}) copy-start(bf16[4,1,64,576]{3,2,1,0:T(8,128)(2,1)S(1)} %all-to-all-done.1) | copy-start | bytes 884740
  32.8 10.9 %all-to-all-start.3 = ((bf16[4,1,64,576]{3,2,1,0:T(8,128)(2,1)}), bf16[4,1,64,576]{3,2,1,0:T(8,128)(2,1)S(1)}, u32[]{:S(2)}, u32[]{:S(2)}) async-start(bf16[4,1,64,576]{3,2,1,0:T(8,128)(2,1)} %bitcast.6), calls=%async_computation.3 | async-start | bytes 655360 | tf_op jit(solution)/shard_map/all_to_all | solution.py:39
  43.7 0.7 copy-start.2
  44.4 53.1 %all-to-all-start.4 = ((bf16[128,128,128]{2,1,0:T(8,128)(2,1)}), bf16[128,128,128]{2,1,0:T(8,128)(2,1)}, u32[]{:S(2)}, u32[]{:S(2)}) async-start(bf16[128,128,128]{2,1,0:T(8,128)(2,1)} %param.7), calls=%async_computation.4 | async-start | bytes 8388608 | tf_op jit(solution)/shard_map/all_to_all | solution.py:58
  51.3 3.1 %copy-start.3 = (bf16[4,1,64,576]{3,2,1,0:T(8,128)(2,1)S(1)}, bf16[4,1,64,576]{3,2,1,0:T(8,128)(2,1)}, u32[]{:S(2)}) copy-start(bf16[4,1,64,576]{3,2,1,0:T(8,128)(2,1)} %copy-done.2) | copy-start | bytes 884740
  61.8 2.3 %copy-start.5 = (bf16[4,64,576]{2,1,0:T(8,128)(2,1)S(1)}, bf16[4,64,576]{2,1,0:T(8,128)(2,1)}, u32[]{:S(2)}) copy-start(bf16[4,64,576]{2,1,0:T(8,128)(2,1)} %gather_fusion.1) | copy-start | bytes 884740
  64.1 1.0 copy-start.4
where the time goes:
time: 103 us; the launch traced here: 102 us
  waiting for transfers between devices  51.5 us (50%)
  starting transfers between devices  21.5 us (21%)
  local copies, waits for them, and re-layouts  16.6 us (16%)
  blocking collectives  4.81 us (5%)
  matrix products  4.57 us (4%)
  other arithmetic  2.85 us (3%)
    all_to_all x1, waiting for transfers between devices, per_device(): lax.all_to_all(value_up, ('wt', 'sub'), split_axis=0, concat_axis=1, tile...  30 us
    all_to_all x2, waiting for transfers between devices, serve(): lax.all_to_all(latent_cache[safe], 'ctx', split_axis=0, concat_axis=0, ti...  12.7 us
    all_to_all x2, starting transfers between devices, fetch(): lax.all_to_all(mine.reshape(owners, count), 'ctx', split_axis=0, concat_a...  9.57 us
    all_to_all x2, waiting for transfers between devices, fetch(): lax.all_to_all(mine.reshape(owners, count), 'ctx', split_axis=0, concat_a...  8.76 us
    all_to_all x2, starting transfers between devices, serve(): lax.all_to_all(latent_cache[safe], 'ctx', split_axis=0, concat_axis=0, ti...  7.06 us
    all_to_all x1, starting transfers between devices, per_device(): lax.all_to_all(value_up, ('wt', 'sub'), split_axis=0, concat_axis=1, tile...  4.86 us
    all_gather x2, blocking collectives, fetch(): fetched = lax.all_gather(fetched, 'sub', axis=2, tiled=True)  4.81 us
    slice x1, local copies, waits for them, and re-layouts, per_device(): queries[index]  3.08 us
  transfers between devices with their start and end apart: 5, of which 5 were waited for; matrix products, arithmetic and copies ran while one was open for 17% of the time, Pallas kernels for 0%

commit v1 on v0

--- a/solution.py
+++ b/solution.py
@@ -6,6 +6,18 @@
 LAT = 512
 ROPE = 64
 NOPE = 128
+
+
+def sent_to_each(value, axis, split, join):
+    ways, here = (lax.axis_size(axis), lax.axis_index(axis))
+    width = value.shape[split] // ways
+    turned = jnp.roll(value, -here * width, axis=split)
+    got = [lax.slice_in_dim(turned, 0, width, axis=split)]
+    for far in range(1, ways):
+        sent = lax.slice_in_dim(turned, far * width, (far + 1) * width, axis=split)
+        got.append(lax.ppermute(sent, axis, [(d, (d + far) % ways) for d in range(ways)]))
+    line = jnp.concatenate(got[::-1], axis=join)
+    return jnp.roll(line, (here + 1) * got[0].shape[join], axis=join)
 
 
 def attend(query, blocks, chosen):
@@ -42,11 +54,7 @@
         half = slots // 2
         mine = lax.dynamic_slice_in_dim(wanted, lax.axis_index("sub") * half, half, 2)
         count = mine.shape[1] * mine.shape[2]
-        fetched = serve(
-            lax.all_to_all(
-                mine.reshape(owners, count), "ctx", split_axis=0, concat_axis=0, tiled=True
-            )
-        )
+        fetched = serve(sent_to_each(mine.reshape(owners, count), "ctx", 0, 0))
         fetched = fetched.reshape(owners, mine.shape[1], mine.shape[2], block_len, width)
         fetched = lax.all_gather(fetched, "sub", axis=2, tiled=True)
         return fetched

time: 103 us -> 105 us (1.019)
  waiting for transfers between devices: 51.5 us -> 45.7 us
  other arithmetic: 2.85 us -> 7.87 us
  starting transfers between devices: 21.5 us -> 24.3 us
    ppermute x0 -> x6, starting transfers between devices: none -> 11 us  [sent_to_each(): lax.ppermute(sent, axis, [(d, (d + far) % ways) for d in range(ways)])]
    all_to_all x2 -> x0, starting transfers between devices: 9.57 us -> none  [fetch(): lax.all_to_all(mine.reshape(owners, count), 'ctx', split_axis=0, concat_a...]
    ppermute x0 -> x6, waiting for transfers between devices: none -> 8.77 us  [sent_to_each(): lax.ppermute(sent, axis, [(d, (d + far) % ways) for d in range(ways)])]
    all_to_all x2 -> x0, waiting for transfers between devices: 8.76 us -> none  [fetch(): lax.all_to_all(mine.reshape(owners, count), 'ctx', split_axis=0, concat_a...]
    all_to_all x2, waiting for transfers between devices: 12.7 us -> 6.94 us  [serve(): lax.all_to_all(latent_cache[safe], 'ctx', split_axis=0, concat_axis=0, ti...]
    concatenate x0 -> x4, other arithmetic: none -> 5.19 us  [the longest x2 5.04 us: sent_to_each(): return jnp.roll(line, (here + 1) * got[0].shape[join], axis=join)]
    all_to_all x2, starting transfers between devices: 7.06 us -> 8.38 us  [serve(): lax.all_to_all(latent_cache[safe], 'ctx', split_axis=0, concat_axis=0, ti...]
    slice x0 -> x2, local copies, waits for them, and re-layouts: none -> 1.28 us  [sent_to_each(): sent = lax.slice_in_dim(turned, far * width, (far + 1) * width, axis=split)]
  transfers between devices with their start and end apart: 5 -> 9, of which waited for: 5 -> 6; matrix products, arithmetic and copies ran while one was open for 17% -> 17% of each run, Pallas kernels for 0% -> 0%
where the time goes in v1:
time: 105 us; the launch traced here: 104 us
  waiting for transfers between devices  45.7 us (44%)
  starting transfers between devices  24.3 us (23%)
  local copies, waits for them, and re-layouts  16.6 us (16%)
  other arithmetic  7.87 us (7%)
  blocking collectives  4.81 us (5%)
  matrix products  4.56 us (4%)
    all_to_all x1, waiting for transfers between devices, per_device(): lax.all_to_all(value_up, ('wt', 'sub'), split_axis=0, concat_axis=1, tile...  30 us
    ppermute x6, starting transfers between devices, sent_to_each(): lax.ppermute(sent, axis, [(d, (d + far) % ways) for d in range(ways)])  11 us
    ppermute x6, waiting for transfers between devices, sent_to_each(): lax.ppermute(sent, axis, [(d, (d + far) % ways) for d in range(ways)])  8.77 us
    all_to_all x2, starting transfers between devices, serve(): lax.all_to_all(latent_cache[safe], 'ctx', split_axis=0, concat_axis=0, ti...  8.38 us
    all_to_all x2, waiting for transfers between devices, serve(): lax.all_to_all(latent_cache[safe], 'ctx', split_axis=0, concat_axis=0, ti...  6.94 us
    concatenate x2, other arithmetic, sent_to_each(): return jnp.roll(line, (here + 1) * got[0].shape[join], axis=join)  5.04 us
    all_to_all x1, starting transfers between devices, per_device(): lax.all_to_all(value_up, ('wt', 'sub'), split_axis=0, concat_axis=1, tile...  4.86 us
    all_gather x2, blocking collectives, fetch(): fetched = lax.all_gather(fetched, 'sub', axis=2, tiled=True)  4.81 us
  transfers between devices with their start and end apart: 9, of which 6 were waited for; matrix products, arithmetic and copies ran while one was open for 17% of the time, Pallas kernels for 0%

profile of v1, /device:TPU:0, one launch (start us, length us, event | category | flops | bytes accessed | tf_op | source)
XLA Modules:
  0.0 104.1 jit_solution(8502659693356152239)
XLA Ops:
  0.0 0.8 fusion.17
  0.8 0.1 pad_add_fusion.1
  0.9 0.1 constant_dynamic-slice_fusion
  1.0 0.6 fusion.19
  1.6 5.1 %collective-permute-start.3 = (s32[1,1]{0,1:T(1,128)}, s32[1,1]{0,1:T(1,128)}, u32[]{:S(2)}, u32[]{:S(2)}) collective-permute-start(s32[1,1]{0,1:T(1,128)} %get-tuple-element.20), channel_id=1, source_target_pairs={{0,12},{4,0},{8,4},{12,8},{1,13},{5,1},{9,5},{13,9},{2,14},{6,2},{... | collective-permute-start | bytes 20 | tf_op jit(solution)/shard_map/ppermute | solution.py:18
  6.7 1.0 collective-permute-start.4
  7.8 0.3 collective-permute-done.3
  8.1 4.1 %collective-permute-done.5 = s32[1,1]{0,1:T(1,128)} collective-permute-done((s32[1,1]{0,1:T(1,128)}, s32[1,1]{0,1:T(1,128)}, u32[]{:S(2)}, u32[]{:S(2)}) %collective-permute-start.5) | collective-permute-done | bytes 36 | tf_op jit(solution)/shard_map/ppermute | solution.py:18
  12.2 2.6 %add_add_fusion.1 = s32[8,1]{0,1:T(1,128)S(1)} fusion(s32[1,1]{0,1:T(1,128)} %get-tuple-element.21, s32[1,1]{0,1:T(1,128)} %collective-permute-done.5, s32[1,1]{0,1:T(1,128)} %collective-permute-done.4, s32[1,1]{0,1:T(1,128)} %collective-permute-done.3), kind=kLoop, calls=%fused_computation.43 | loop fusion | flops 56 | bytes 48 | tf_op jit(solution)/shard_map/jit(_roll_dynamic)/concatenate | solution.py:20
  14.8 0.1 fusion.15
  14.9 1.3 %gather_fusion.2 = bf16[4,64,576]{2,1,0:T(8,128)(2,1)} fusion(bf16[16,64,576]{2,1,0:T(8,128)(2,1)S(1)} %copy-done, s32[1024]{0:T(1024)S(1)} %pad_clamp_fusion.1), kind=kCustom, calls=%fused_computation.2 | custom fusion | bytes 589840 | tf_op jit(solution)/shard_map/gather | solution.py:51
  16.2 4.2 %all-to-all-start.1 = ((bf16[4,1,64,576]{3,2,1,0:T(8,128)(2,1)}), bf16[4,1,64,576]{3,2,1,0:T(8,128)(2,1)S(1)}, u32[]{:S(2)}, u32[]{:S(2)}) async-start(bf16[4,1,64,576]{3,2,1,0:T(8,128)(2,1)} %bitcast.10), calls=%async_computation.1 | async-start | bytes 655360 | tf_op jit(solution)/shard_map/all_to_all | solution.py:51
  20.4 0.7 fusion.18
  21.1 3.8 %collective-permute-start = (s32[1,1]{0,1:T(1,128)}, s32[1,1]{0,1:T(1,128)}, u32[]{:S(2)}, u32[]{:S(2)}) collective-permute-start(s32[1,1]{0,1:T(1,128)} %get-tuple-element.16), channel_id=1, source_target_pairs={{0,12},{4,0},{8,4},{12,8},{1,13},{5,1},{9,5},{13,9},{2,14},{6,2},{... | collective-permute-start | bytes 20 | tf_op jit(solution)/shard_map/ppermute | solution.py:18
  24.9 1.1 %collective-permute-start.1 = (s32[1,1]{0,1:T(1,128)}, s32[1,1]{0,1:T(1,128)}, u32[]{:S(2)}, u32[]{:S(2)}) collective-permute-start(s32[1,1]{0,1:T(1,128)} %get-tuple-element.19), channel_id=1, source_target_pairs={{0,8},{4,12},{8,0},{12,4},{1,9},{5,13},{9,1},{13,5},{2,10},{6,14},... | collective-permute-start | bytes 20 | tf_op jit(solution)/shard_map/ppermute | solution.py:18
  26.0 0.2 collective-permute-done
  26.3 4.2 %collective-permute-done.2 = s32[1,1]{0,1:T(1,128)} collective-permute-done((s32[1,1]{0,1:T(1,128)}, s32[1,1]{0,1:T(1,128)}, u32[]{:S(2)}, u32[]{:S(2)}) %collective-permute-start.2) | collective-permute-done | bytes 36 | tf_op jit(solution)/shard_map/ppermute | solution.py:18
  30.4 2.4 %add_add_fusion = s32[8,1]{0,1:T(1,128)S(1)} fusion(s32[1,1]{0,1:T(1,128)} %get-tuple-element.17, s32[1,1]{0,1:T(1,128)} %collective-permute-done.2, s32[1,1]{0,1:T(1,128)} %collective-permute-done.1, s32[1,1]{0,1:T(1,128)} %collective-permute-done), kind=kLoop, calls=%fused_computation.41 | loop fusion | flops 56 | bytes 48 | tf_op jit(solution)/shard_map/jit(_roll_dynamic)/concatenate | solution.py:20
  32.9 0.1 fusion.14
  32.9 1.3 %gather_fusion = bf16[4,64,576]{2,1,0:T(8,128)(2,1)} fusion(bf16[16,64,576]{2,1,0:T(8,128)(2,1)S(1)} %copy-done, s32[1024]{0:T(1024)S(1)} %pad_clamp_fusion.3), kind=kCustom, calls=%fused_computation | custom fusion | bytes 589840 | tf_op jit(solution)/shard_map/gather | solution.py:51
  34.2 4.2 %all-to-all-start = ((bf16[4,1,64,576]{3,2,1,0:T(8,128)(2,1)}), bf16[4,1,64,576]{3,2,1,0:T(8,128)(2,1)S(1)}, u32[]{:S(2)}, u32[]{:S(2)}) async-start(bf16[4,1,64,576]{3,2,1,0:T(8,128)(2,1)} %bitcast.3), calls=%async_computation | async-start | bytes 655360 | tf_op jit(solution)/shard_map/all_to_all | solution.py:51
  38.5 0.1 copy.10
  38.5 0.1 select_n.42
  38.6 0.1 copy.11
  38.7 0.1 select_n.46
  38.8 6.9 %all-to-all-done = bf16[4,1,64,576]{3,2,1,0:T(8,128)(2,1)S(1)} async-done(((bf16[4,1,64,576]{3,2,1,0:T(8,128)(2,1)}), bf16[4,1,64,576]{3,2,1,0:T(8,128)(2,1)S(1)}, u32[]{:S(2)}, u32[]{:S(2)}) %all-to-all-start) | async-done | bytes 294944 | tf_op jit(solution)/shard_map/all_to_all | solution.py:51
  45.7 0.7 copy-done.2
  46.5 4.9 %all-to-all-start.2 = ((bf16[128,128,128]{2,1,0:T(8,128)(2,1)}), bf16[128,128,128]{2,1,0:T(8,128)(2,1)}, u32[]{:S(2)}, u32[]{:S(2)}) async-start(bf16[128,128,128]{2,1,0:T(8,128)(2,1)} %param.9), calls=%async_computation.2 | async-start | bytes 8388608 | tf_op jit(solution)/shard_map/all_to_all | solution.py:66
  51.4 1.0 sort.31
  52.4 1.0 sort.32
  53.4 3.1 %fusion.16 = (bf16[1,32,32,576]{3,2,1,0:T(8,128)(2,1)S(1)}, bf16[1,32,32,576]{3,2,1,0:T(8,128)(2,1)}) fusion(bf16[2,32,32,576]{3,2,1,0:T(8,128)(2,1)} %param.6), kind=kLoop, calls=%fused_computation.48 | loop fusion | bytes 4718592 | tf_op jit(solution)/shard_map/slice | solution.py:64
  56.5 2.3 %all-gather = bf16[4,2,64,576]{3,2,1,0:T(8,128)(2,1)S(1)} all-gather(bf16[4,1,64,576]{3,2,1,0:T(8,128)(2,1)S(1)} %copy-done.3), channel_id=2, replica_groups=mesh['groups'=2,'ctx'=4,'wt'=2,'sub'=2] {'sub'}, dimensions={1}, use_global_device_ids=true | all-gather | bytes 884736 | tf_op jit(solution)/shard_map/all_gather | solution.py:59
  58.8 1.3 %gather_fusion.1 = bf16[4,64,576]{2,1,0:T(8,128)(2,1)} fusion(bf16[8,64,576]{2,1,0:T(8,128)(2,1)S(1)} %bitcast.38, s32[1024]{0:T(1024)S(1)} %pad_clamp_fusion.2), kind=kCustom, calls=%fused_computation.1 | custom fusion | bytes 589840 | tf_op jit(solution)/shard_map/gather | solution.py:30
  60.1 2.5 %all-gather.1 = bf16[4,2,64,576]{3,2,1,0:T(8,128)(2,1)S(1)} all-gather(bf16[4,1,64,576]{3,2,1,0:T(8,128)(2,1)} %copy-done.1), channel_id=3, replica_groups=mesh['groups'=2,'ctx'=4,'wt'=2,'sub'=2] {'sub'}, dimensions={1}, use_global_device_ids=true | all-gather | bytes 884736 | tf_op jit(solution)/shard_map/all_gather | solution.py:59
  62.6 1.3 %gather_fusion.3 = bf16[4,64,576]{2,1,0:T(8,128)(2,1)} fusion(bf16[8,64,576]{2,1,0:T(8,128)(2,1)S(1)} %bitcast.39, s32[1024]{0:T(1024)S(1)} %pad_clamp_fusion), kind=kCustom, calls=%fused_computation.3 | custom fusion | bytes 589840 | tf_op jit(solution)/shard_map/gather | solution.py:30
  63.9 2.1 %fusion.20 = (f32[1024]{0:T(1024)S(1)}, f32[256,1024]{1,0:T(8,128)S(1)}) fusion(bf16[256,576]{1,0:T(8,128)(2,1)} %bitcast.42, bf16[1024,576]{1,0:T(8,128)(2,1)} %bitcast.36), kind=kOutput, calls=%fused_computation.52 | convolution fusion | flops 302513152 | bytes 2527232 | tf_op jit(solution)/shard_map/rd,kd->rk/dot_general | solution.py:32
  66.0 0.2 fusion.2
  66.2 0.6 fusion.21
  66.8 0.2 fusion
  67.0 0.1 copy-done.5
  67.2 0.5 divide_convert_fusion
  67.7 0.5 divide_convert_fusion.1
  68.2 0.2 pad_maximum_fusion
  68.4 1.2 %copy.12 = bf16[2,32,32,512]{3,1,0,2:T(8,128)(2,1)S(1)} copy(bf16[2,32,32,512]{3,2,1,0:T(8,128)(2,1)S(1)} %pad_maximum_fusion) | data formatting | bytes 4194304 | tf_op jit(solution)/shard_map/stack | solution.py:65
  69.5 30.0 %all-to-all-done.2 = bf16[128,128,128]{2,1,0:T(8,128)(2,1)} async-done(((bf16[128,128,128]{2,1,0:T(8,128)(2,1)}), bf16[128,128,128]{2,1,0:T(8,128)(2,1)}, u32[]{:S(2)}, u32[]{:S(2)}) %all-to-all-start.2) | async-done | bytes 4194336 | tf_op jit(solution)/shard_map/all_to_all | solution.py:66
  99.6 2.5 %copy.13 = bf16[4,32,128,128]{3,2,0,1:T(8,128)(2,1)S(1)} copy(bf16[4,32,128,128]{3,2,1,0:T(8,128)(2,1)} %bitcast.16) | data formatting | bytes 8388608 | tf_op jit(solution)/shard_map/all_to_all | solution.py:66
  102.1 0.9 convolution_convert_fusion
  102.9 1.1 %copy.14 = bf16[2,32,32,128]{3,2,1,0:T(8,128)(2,1)} copy(bf16[2,32,32,128]{3,1,0,2:T(8,128)(2,1)S(1)} %bitcast.37) | data formatting | bytes 1048576 | tf_op jit(solution)/shard_map/reshape | solution.py:68
  (31 shorter events, 0.2 us)
Async XLA Ops:
  0.0 14.9 %copy-start = (bf16[16,64,576]{2,1,0:T(8,128)(2,1)S(1)}, bf16[16,64,576]{2,1,0:T(8,128)(2,1)}, u32[]{:S(2)}) copy-start(bf16[16,64,576]{2,1,0:T(8,128)(2,1)} %param.8) | copy-start | bytes 3538948
  0.0 38.4 %copy-start.6 = (s32[2,4,2]{1,2,0:T(2,128)S(1)}, s32[2,4,2]{1,2,0:T(2,128)}, u32[]{:S(2)}) copy-start(s32[2,4,2]{1,2,0:T(2,128)} %param.7) | copy-start | bytes 196
  1.6 6.5 %collective-permute-start.3 = (s32[1,1]{0,1:T(1,128)}, s32[1,1]{0,1:T(1,128)}, u32[]{:S(2)}, u32[]{:S(2)}) collective-permute-start(s32[1,1]{0,1:T(1,128)} %get-tuple-element.20), channel_id=1, source_target_pairs={{0,12},{4,0},{8,4},{12,8},{1,13},{5,1},{9,5},{13,9},{2,14},{6,2},{... | collective-permute-start | bytes 20 | tf_op jit(solution)/shard_map/ppermute | solution.py:18
  6.7 5.5 %collective-permute-start.5 = (s32[1,1]{0,1:T(1,128)}, s32[1,1]{0,1:T(1,128)}, u32[]{:S(2)}, u32[]{:S(2)}) collective-permute-start(s32[1,1]{0,1:T(1,128)} %get-tuple-element.22), channel_id=1, source_target_pairs={{0,4},{4,8},{8,12},{12,0},{1,5},{5,9},{9,13},{13,1},{2,6},{6,10},{... | collective-permute-start | bytes 20 | tf_op jit(solution)/shard_map/ppermute | solution.py:18
  6.7 5.5 %collective-permute-start.4 = (s32[1,1]{0,1:T(1,128)}, s32[1,1]{0,1:T(1,128)}, u32[]{:S(2)}, u32[]{:S(2)}) collective-permute-start(s32[1,1]{0,1:T(1,128)} %get-tuple-element.23), channel_id=1, source_target_pairs={{0,8},{4,12},{8,0},{12,4},{1,9},{5,13},{9,1},{13,5},{2,10},{6,14},... | collective-permute-start | bytes 20 | tf_op jit(solution)/shard_map/ppermute | solution.py:18
  16.2 18.0 %all-to-all-start.1 = ((bf16[4,1,64,576]{3,2,1,0:T(8,128)(2,1)}), bf16[4,1,64,576]{3,2,1,0:T(8,128)(2,1)S(1)}, u32[]{:S(2)}, u32[]{:S(2)}) async-start(bf16[4,1,64,576]{3,2,1,0:T(8,128)(2,1)} %bitcast.10), calls=%async_computation.1 | async-start | bytes 655360 | tf_op jit(solution)/shard_map/all_to_all | solution.py:51
  21.1 5.2 %collective-permute-start = (s32[1,1]{0,1:T(1,128)}, s32[1,1]{0,1:T(1,128)}, u32[]{:S(2)}, u32[]{:S(2)}) collective-permute-start(s32[1,1]{0,1:T(1,128)} %get-tuple-element.16), channel_id=1, source_target_pairs={{0,12},{4,0},{8,4},{12,8},{1,13},{5,1},{9,5},{13,9},{2,14},{6,2},{... | collective-permute-start | bytes 20 | tf_op jit(solution)/shard_map/ppermute | solution.py:18
  24.9 5.5 %collective-permute-start.2 = (s32[1,1]{0,1:T(1,128)}, s32[1,1]{0,1:T(1,128)}, u32[]{:S(2)}, u32[]{:S(2)}) collective-permute-start(s32[1,1]{0,1:T(1,128)} %get-tuple-element.18), channel_id=1, source_target_pairs={{0,4},{4,8},{8,12},{12,0},{1,5},{5,9},{9,13},{13,1},{2,6},{6,10},{... | collective-permute-start | bytes 20 | tf_op jit(solution)/shard_map/ppermute | solution.py:18
  24.9 5.5 %collective-permute-start.1 = (s32[1,1]{0,1:T(1,128)}, s32[1,1]{0,1:T(1,128)}, u32[]{:S(2)}, u32[]{:S(2)}) collective-permute-start(s32[1,1]{0,1:T(1,128)} %get-tuple-element.19), channel_id=1, source_target_pairs={{0,8},{4,12},{8,0},{12,4},{1,9},{5,13},{9,1},{13,5},{2,10},{6,14},... | collective-permute-start | bytes 20 | tf_op jit(solution)/shard_map/ppermute | solution.py:18
  34.2 11.5 %copy-start.1 = (bf16[4,1,64,576]{3,2,1,0:T(8,128)(2,1)}, bf16[4,1,64,576]{3,2,1,0:T(8,128)(2,1)S(1)}, u32[]{:S(2)}) copy-start(bf16[4,1,64,576]{3,2,1,0:T(8,128)(2,1)S(1)} %all-to-all-done.1) | copy-start | bytes 884740
  34.2 11.5 %all-to-all-start = ((bf16[4,1,64,576]{3,2,1,0:T(8,128)(2,1)}), bf16[4,1,64,576]{3,2,1,0:T(8,128)(2,1)S(1)}, u32[]{:S(2)}, u32[]{:S(2)}) async-start(bf16[4,1,64,576]{3,2,1,0:T(8,128)(2,1)} %bitcast.3), calls=%async_computation | async-start | bytes 655360 | tf_op jit(solution)/shard_map/all_to_all | solution.py:51
  45.7 0.8 copy-start.2
  46.5 53.1 %all-to-all-start.2 = ((bf16[128,128,128]{2,1,0:T(8,128)(2,1)}), bf16[128,128,128]{2,1,0:T(8,128)(2,1)}, u32[]{:S(2)}, u32[]{:S(2)}) async-start(bf16[128,128,128]{2,1,0:T(8,128)(2,1)} %param.9), calls=%async_computation.2 | async-start | bytes 8388608 | tf_op jit(solution)/shard_map/all_to_all | solution.py:66
  53.4 3.1 %copy-start.3 = (bf16[4,1,64,576]{3,2,1,0:T(8,128)(2,1)S(1)}, bf16[4,1,64,576]{3,2,1,0:T(8,128)(2,1)}, u32[]{:S(2)}) copy-start(bf16[4,1,64,576]{3,2,1,0:T(8,128)(2,1)} %copy-done.2) | copy-start | bytes 884740
  63.9 2.3 %copy-start.4 = (bf16[4,64,576]{2,1,0:T(8,128)(2,1)S(1)}, bf16[4,64,576]{2,1,0:T(8,128)(2,1)}, u32[]{:S(2)}) copy-start(bf16[4,64,576]{2,1,0:T(8,128)(2,1)} %gather_fusion.1) | copy-start | bytes 884740
  66.2 1.0 copy-start.5
